TPU v7x, 32 devices: a whole 2x2x4 slice. The times are simulated.
32 devices in a mesh: group: 4 (over y, core), member: 8 (over z, x).
Axes of the slice: x: 2, y: 2, z: 4, core: 2. Of those that a mesh axis runs over, the one named last changes fastest.
Arguments:
- position: float32 [3, 262144], P(None, ('group', 'member')), may hold values from -6 to 6
- velocity: float32 [3, 262144], P(None, ('group', 'member')), may hold values from -6 to 6
- mass: float32 [262144], P(('group', 'member')), may hold values from 0.0009765625 to 0.0078125
- neighbours: int32 [2048, 4], P(('group', 'member')), may hold values from 0 to 71
- list_length: int32 [2048], P(('group', 'member')), may hold values from 1 to 4
- let_list: int32 [32, 8], P(('group', 'member')), may hold values from 0 to 63
- cell_list: int32 [32, 32], P(('group', 'member')), may hold values from 0 to 511
- destination: int32 [2, 2048], P(None, ('group', 'member')), may hold values from 0 to 7, as said below
Outputs:
- final_position: float32 [3, 262144], P(None, ('group', 'member'))
- final_velocity: float32 [3, 262144], P(None, ('group', 'member'))
- final_mass: float32 [262144], P(('group', 'member'))
Inputs may be any that keep to these rules, and one draw needn't show every extreme that they name: `neighbours`: index into the pool of the block's device: its 64 own blocks, then one block from each member of its group in member order. Only the first list_length entries of a block's list are used. `destination`: in each step and group, all devices move the block in slot b the same number of places along member, wrapping around, so every device receives exactly one block for each slot; a device sends at most 8 blocks to one device, and in every step and group some device sends exactly that many to one device.
All inputs are finite; a program needn't handle non-finite values.
Results may differ from a plain program's by a relative error of at most 0.0003.
Values sent between devices are 32-bit elements; how exact they have to be, the bound alone decides.
A program may use at most 64 MiB of HBM per device.

v0:
```python
import jax
import jax.numpy as jnp
from jax import lax
from jax.sharding import PartitionSpec as P

BLOCK = 128
NB = 64
CELL = 16
LIST = 4
MSEND = 32


SOFTENING = 0.01
TIMESTEP = 0.1


def pull_toward(targets, sources):
    offset = sources[:3, :, None] - targets[:, None, :]
    radius_sq = jnp.sum(offset * offset, axis=0) + SOFTENING
    inverse = lax.rsqrt(radius_sq)
    weight = sources[3][:, None] * inverse * inverse * inverse
    return jnp.sum(offset * weight[None], axis=1)


def in_groups(per_block, targets, extras):
    group_count = targets.shape[1] // 4
    target_groups = jnp.moveaxis(targets.reshape(3, group_count, 4, BLOCK), 1, 0)
    extra_groups = tuple(
        (extra_array.reshape((group_count, 4) + extra_array.shape[1:]) for extra_array in extras)
    )

    def run_group(items):
        return jax.vmap(per_block, in_axes=(1,) + (0,) * len(extras), out_axes=1)(
            items[0], *items[1]
        )

    results = lax.map(run_group, (target_groups, extra_groups))
    return jnp.moveaxis(results, 0, 1).reshape(3, -1, BLOCK)


def forces(coords, masses, neighbours, list_length, let_list, cell_list):
    local_blocks = jnp.concatenate([coords, masses[None]], axis=0)
    outgoing = local_blocks[:, let_list[0]]
    incoming = lax.all_to_all(outgoing, "member", split_axis=1, concat_axis=1, tiled=True)
    source_pool = jnp.concatenate([local_blocks, incoming], axis=1)
    cell_mass = masses.reshape(-1, CELL).sum(1)
    cell_centre = (coords * masses[None]).reshape(3, -1, CELL).sum(2) / cell_mass
    picked = cell_list[0]
    published = jnp.concatenate([cell_centre[:, picked], cell_mass[picked][None]], axis=0)
    own_group = lax.axis_index("group")
    piece = lax.all_gather(published, "group", axis=1, tiled=True)
    columns = jnp.arange(piece.shape[1], dtype=jnp.int32)
    kept_mass = piece[3] * (columns // MSEND != own_group).astype(piece.dtype)
    sources = jnp.concatenate([piece[:3], kept_mass[None]], axis=0)

    def far_block(block_targets):
        return pull_toward(block_targets, sources)

    far_field = in_groups(far_block, coords, ())

    def near_block(block_targets, block_list, block_length):
        chosen = source_pool[:, block_list]
        live = (jnp.arange(LIST, dtype=jnp.int32) < block_length).astype(chosen.dtype)
        sources = jnp.concatenate([chosen[:3], (chosen[3] * live[:, None])[None]], axis=0).reshape(
            4, -1
        )
        return pull_toward(block_targets, sources)

    near_part = in_groups(near_block, coords, (neighbours, list_length))
    return near_part + far_field


def relocate(block_state, target_member):
    members = lax.axis_size("member")
    capacity = (NB + members - 1) // members
    slot_numbers = jnp.arange(NB, dtype=jnp.int32)
    earlier = slot_numbers[None, :] < slot_numbers[:, None]
    same_target = target_member[None, :] == target_member[:, None]
    position_rank = jnp.sum(same_target & earlier, axis=1)
    slot_index = target_member * capacity + position_rank
    places = jnp.arange(members * capacity, dtype=jnp.int32)
    placing = (places[:, None] == slot_index[None, :]).astype(jnp.float32)
    outgoing = jnp.einsum("sb,rbc->rsc", placing, block_state, precision=lax.Precision.HIGHEST)
    slot_labels = (slot_numbers + 1).astype(jnp.float32)
    labels = jnp.dot(placing, slot_labels, precision=lax.Precision.HIGHEST)[None]
    incoming, arrived = (
        lax.all_to_all(outgoing, "member", split_axis=1, concat_axis=1, tiled=True),
        lax.all_to_all(labels, "member", split_axis=1, concat_axis=1, tiled=True),
    )
    landing = (arrived[0][None, :] == slot_labels[:, None]).astype(jnp.float32)
    return jnp.einsum("bs,rsc->rbc", landing, incoming, precision=lax.Precision.HIGHEST)


def shards(position, velocity, mass, neighbours, list_length, let_list, cell_list, destination):
    block_state = jnp.concatenate([position, velocity, mass[None]], axis=0).reshape(7, NB, BLOCK)
    for turn_index in range(2):
        masses = block_state[6]
        coords = block_state[0:3] + 0.5 * TIMESTEP * block_state[3:6]
        acceleration = forces(coords, masses, neighbours, list_length, let_list, cell_list)
        speeds = block_state[3:6] + TIMESTEP * acceleration
        coords = coords + 0.5 * TIMESTEP * speeds
        block_state = jnp.concatenate([coords, speeds, masses[None]], axis=0)
        block_state = relocate(block_state, destination[turn_index])
    flattened = block_state.reshape(7, NB * BLOCK)
    return (flattened[0:3], flattened[3:6], flattened[6])


def solution(mesh):
    return jax.shard_map(
        shards,
        mesh=mesh,
        in_specs=(
            P(None, ("group", "member")),
            P(None, ("group", "member")),
            P(("group", "member")),
            P(("group", "member"), None),
            P(("group", "member")),
            P(("group", "member"), None),
            P(("group", "member"), None),
            P(None, ("group", "member")),
        ),
        out_specs=(
            P(None, ("group", "member")),
            P(None, ("group", "member")),
            P(("group", "member")),
        ),
        check_vma=False,
    )
```

profile of v0, /device:TPU:0, one launch (start us, length us, event | category | flops | bytes accessed | tf_op | source)
XLA Modules:
  0.0 203.1 jit_solution(16272992146009789380)
XLA Ops:
  3.2 1.2 gather_fusion.2
  4.4 7.3 %all-to-all-start = ((f32[4,8,128]{2,0,1:T(4,128)}), f32[4,8,128]{2,0,1:T(4,128)S(1)}, u32[]{:S(2)}, u32[]{:S(2)}) async-start(f32[4,8,128]{2,0,1:T(4,128)} %bitcast.32), calls=%async_computation | async-start | bytes 32768 | tf_op jit(solution)/shard_map/all_to_all | solution.py:44
  14.4 5.2 %all-gather = f32[4,32,4]{1,2,0:T(4,128)S(1)} all-gather(f32[1,32,4]{1,2,0:T(4,128)S(1)} %maximum_bitcast_fusion), channel_id=1, replica_groups=mesh['group'=4,'member'=8] {'group'}, dimensions={0}, use_global_device_ids=true | all-gather | bytes 2560 | tf_op jit(solution)/shard_map/all_gather | solution.py:51
  19.7 7.7 %while.41 = (s32[]{:T(128)}, f32[16,3,4,128]{3,1,2,0:T(4,128)S(1)}, f32[3,128]{1,0:T(4,128)S(1)}, f32[16,3,4,128]{3,2,1,0:T(4,128)S(1)}, f32[128]{0:T(128)S(1)}, /*index=5*/s32[]{:T(128)}) while((s32[]{:T(128)}, f32[16,3,4,128]{3,1,2,0:T(4,128)S(1)}, f32[3,128]{1,0:T(4,128)S(1)}, f32[16,3,4,128]{3,2,1,0:T(4,128)S(1)}, f32[128]{0:T(128)S(1)}, ...), condition=%wide.region_9.10_spmd, body=%wide.region_6.9_spmd.sunk | while | flops 1374722 | bytes 1111637 | solution.py:37
  28.8 6.0 %all-to-all-start.2 = ((f32[1,8,8]{2,0,1:T(1,128)}), f32[1,8,8]{2,0,1:T(1,128)S(1)}, u32[]{:S(2)}, u32[]{:S(2)}) async-start(f32[1,8,8]{2,0,1:T(1,128)} %bitcast.51), calls=%async_computation.2 | async-start | bytes 8192 | tf_op jit(solution)/shard_map/all_to_all | solution.py:88
  34.9 53.8 %while.40 = (s32[]{:T(128)}, f32[16,3,4,128]{3,1,2,0:T(4,128)S(1)}, s32[16,4,4]{2,1,0:T(4,128)S(1)}, f32[4,72,128]{2,0,1:T(4,128)S(1)}, f32[16,3,4,128]{3,2,1,0:T(4,128)S(1)}, /*index=5*/s32[16,4]{1,0:T(8,128)S(1)}, s32[]{:T(128)}) while((s32[]{:T(128)}, f32[16,3,4,128]{3,1,2,0:T(4,128)S(1)}, s32[16,4,4]{2,1,0:T(4,128)S(1)}, ...), condition=%wide.region_3.4_spmd, body=%wide.region_0.3_spmd.sunk | while | flops 5506642 | bytes 4463253 | solution.py:37
  35.7 1.0 fusion.69
  39.0 1.0 fusion.69
  42.4 1.0 fusion.69
  45.7 1.0 fusion.69
  49.1 1.0 fusion.69
  52.5 1.0 fusion.69
  62.5 1.0 fusion.69
  65.9 1.0 fusion.69
  89.9 6.0 %all-to-all-start.1 = ((f32[7,64,128]{2,0,1:T(8,128)}), f32[7,64,128]{2,0,1:T(8,128)S(1)}, u32[]{:S(2)}, u32[]{:S(2)}) async-start(f32[7,64,128]{2,0,1:T(8,128)} %copy.117), calls=%async_computation.1 | async-start | bytes 524288 | tf_op jit(solution)/shard_map/all_to_all | solution.py:87
  98.0 6.7 %all-to-all-done.1 = f32[7,64,128]{2,0,1:T(8,128)S(1)} async-done(((f32[7,64,128]{2,0,1:T(8,128)}), f32[7,64,128]{2,0,1:T(8,128)S(1)}, u32[]{:S(2)}, u32[]{:S(2)}) %all-to-all-start.1) | async-done | bytes 229408 | tf_op jit(solution)/shard_map/all_to_all | solution.py:87
  105.3 1.2 gather_fusion.5
  106.5 3.6 %all-to-all-start.3 = ((f32[4,8,128]{2,0,1:T(4,128)}), f32[4,8,128]{2,0,1:T(4,128)S(1)}, u32[]{:S(2)}, u32[]{:S(2)}) async-start(f32[4,8,128]{2,0,1:T(4,128)} %bitcast.54), calls=%async_computation.3 | async-start | bytes 32768 | tf_op jit(solution)/shard_map/all_to_all | solution.py:44
  112.4 5.2 %all-gather.1 = f32[4,32,4]{1,2,0:T(4,128)S(1)} all-gather(f32[1,32,4]{1,2,0:T(4,128)S(1)} %maximum_bitcast_fusion.1), channel_id=1, replica_groups=mesh['group'=4,'member'=8] {'group'}, dimensions={0}, use_global_device_ids=true | all-gather | bytes 2560 | tf_op jit(solution)/shard_map/all_gather | solution.py:51
  117.7 7.7 %while.43 = (s32[]{:T(128)}, f32[16,3,4,128]{3,1,2,0:T(4,128)S(1)}, f32[3,128]{1,0:T(4,128)S(1)}, f32[16,3,4,128]{3,2,1,0:T(4,128)S(1)}, f32[128]{0:T(128)S(1)}, /*index=5*/s32[]{:T(128)}) while((s32[]{:T(128)}, f32[16,3,4,128]{3,1,2,0:T(4,128)S(1)}, f32[3,128]{1,0:T(4,128)S(1)}, f32[16,3,4,128]{3,2,1,0:T(4,128)S(1)}, f32[128]{0:T(128)S(1)}, ...), condition=%wide.region_20.21_spmd, body=%wide.region_17.20_spmd.sunk | while | flops 1374722 | bytes 1111637 | solution.py:37
  125.4 6.0 %all-to-all-start.5 = ((f32[1,8,8]{2,0,1:T(1,128)}), f32[1,8,8]{2,0,1:T(1,128)S(1)}, u32[]{:S(2)}, u32[]{:S(2)}) async-start(f32[1,8,8]{2,0,1:T(1,128)} %bitcast.73), calls=%async_computation.5 | async-start | bytes 8192 | tf_op jit(solution)/shard_map/all_to_all | solution.py:88
  131.5 53.8 %while.42 = (s32[]{:T(128)}, f32[16,3,4,128]{3,1,2,0:T(4,128)S(1)}, s32[16,4,4]{2,1,0:T(4,128)S(1)}, f32[4,72,128]{2,0,1:T(4,128)S(1)}, f32[16,3,4,128]{3,2,1,0:T(4,128)S(1)}, /*index=5*/s32[16,4]{1,0:T(8,128)S(1)}, s32[]{:T(128)}) while((s32[]{:T(128)}, f32[16,3,4,128]{3,1,2,0:T(4,128)S(1)}, s32[16,4,4]{2,1,0:T(4,128)S(1)}, ...), condition=%wide.region_14.15_spmd, body=%wide.region_11.14_spmd.sunk | while | flops 5506642 | bytes 4463253 | solution.py:37
  186.5 6.0 %all-to-all-start.4 = ((f32[7,64,128]{2,0,1:T(8,128)}), f32[7,64,128]{2,0,1:T(8,128)S(1)}, u32[]{:S(2)}, u32[]{:S(2)}) async-start(f32[7,64,128]{2,0,1:T(8,128)} %copy.128), calls=%async_computation.4 | async-start | bytes 524288 | tf_op jit(solution)/shard_map/all_to_all | solution.py:87
  193.2 8.1 %all-to-all-done.4 = f32[7,64,128]{2,0,1:T(8,128)S(1)} async-done(((f32[7,64,128]{2,0,1:T(8,128)}), f32[7,64,128]{2,0,1:T(8,128)S(1)}, u32[]{:S(2)}, u32[]{:S(2)}) %all-to-all-start.4) | async-done | bytes 229408 | tf_op jit(solution)/shard_map/all_to_all | solution.py:87
  (765 shorter events, 126.7 us)
Async XLA Ops:
  0.6 11.1 %copy-start.1 = (f32[3,8192]{1,0:T(4,128)S(1)}, f32[3,8192]{1,0:T(4,128)}, u32[]{:S(2)}) copy-start(f32[3,8192]{1,0:T(4,128)} %param.16) | copy-start | bytes 294916
  0.6 11.1 %copy-start = (f32[3,8192]{1,0:T(4,128)S(1)}, f32[3,8192]{1,0:T(4,128)}, u32[]{:S(2)}) copy-start(f32[3,8192]{1,0:T(4,128)} %param.17) | copy-start | bytes 294916
  0.6 11.1 %copy-start.2 = (f32[8192]{0:T(1024)S(1)}, f32[8192]{0:T(1024)}, u32[]{:S(2)}) copy-start(f32[8192]{0:T(1024)} %param.18) | copy-start | bytes 98308
  3.2 9.1 %copy-start.6 = (s32[1,32]{1,0:T(1,128)S(1)}, s32[1,32]{1,0:T(1,128)}, u32[]{:S(2)}) copy-start(s32[1,32]{1,0:T(1,128)} %param.22) | copy-start | bytes 388
  4.4 24.4 %all-to-all-start = ((f32[4,8,128]{2,0,1:T(4,128)}), f32[4,8,128]{2,0,1:T(4,128)S(1)}, u32[]{:S(2)}, u32[]{:S(2)}) async-start(f32[4,8,128]{2,0,1:T(4,128)} %bitcast.32), calls=%async_computation | async-start | bytes 32768 | tf_op jit(solution)/shard_map/all_to_all | solution.py:44
  19.7 7.7 %copy-start.4 = (s32[2,64]{1,0:T(2,128)S(1)}, s32[2,64]{1,0:T(2,128)}, u32[]{:S(2)}) copy-start(s32[2,64]{1,0:T(2,128)} %param.23) | copy-start | bytes 1540
  19.7 8.2 %copy-start.3 = (s32[64,4]{0,1:T(4,128)S(1)}, s32[64,4]{0,1:T(4,128)}, u32[]{:S(2)}) copy-start(s32[64,4]{0,1:T(4,128)} %param.19) | copy-start | bytes 3076
  19.7 8.4 %copy-start.5 = (s32[64]{0:T(128)S(1)}, s32[64]{0:T(128)}, u32[]{:S(2)}) copy-start(s32[64]{0:T(128)} %param.20) | copy-start | bytes 772
  28.8 61.1 %all-to-all-start.2 = ((f32[1,8,8]{2,0,1:T(1,128)}), f32[1,8,8]{2,0,1:T(1,128)S(1)}, u32[]{:S(2)}, u32[]{:S(2)}) async-start(f32[1,8,8]{2,0,1:T(1,128)} %bitcast.51), calls=%async_computation.2 | async-start | bytes 8192 | tf_op jit(solution)/shard_map/all_to_all | solution.py:88
  89.9 14.9 %all-to-all-start.1 = ((f32[7,64,128]{2,0,1:T(8,128)}), f32[7,64,128]{2,0,1:T(8,128)S(1)}, u32[]{:S(2)}, u32[]{:S(2)}) async-start(f32[7,64,128]{2,0,1:T(8,128)} %copy.117), calls=%async_computation.1 | async-start | bytes 524288 | tf_op jit(solution)/shard_map/all_to_all | solution.py:87
  106.5 18.8 %all-to-all-start.3 = ((f32[4,8,128]{2,0,1:T(4,128)}), f32[4,8,128]{2,0,1:T(4,128)S(1)}, u32[]{:S(2)}, u32[]{:S(2)}) async-start(f32[4,8,128]{2,0,1:T(4,128)} %bitcast.54), calls=%async_computation.3 | async-start | bytes 32768 | tf_op jit(solution)/shard_map/all_to_all | solution.py:44
  125.4 61.1 %all-to-all-start.5 = ((f32[1,8,8]{2,0,1:T(1,128)}), f32[1,8,8]{2,0,1:T(1,128)S(1)}, u32[]{:S(2)}, u32[]{:S(2)}) async-start(f32[1,8,8]{2,0,1:T(1,128)} %bitcast.73), calls=%async_computation.5 | async-start | bytes 8192 | tf_op jit(solution)/shard_map/all_to_all | solution.py:88
  186.5 14.9 %all-to-all-start.4 = ((f32[7,64,128]{2,0,1:T(8,128)}), f32[7,64,128]{2,0,1:T(8,128)S(1)}, u32[]{:S(2)}, u32[]{:S(2)}) async-start(f32[7,64,128]{2,0,1:T(8,128)} %copy.128), calls=%async_computation.4 | async-start | bytes 524288 | tf_op jit(solution)/shard_map/all_to_all | solution.py:87
where the time goes:
time: 204 us; the launch traced here: 203 us
  other arithmetic  99.9 us (49%)
  local copies, waits for them, and re-layouts  36.1 us (18%)
  starting transfers between devices  34.8 us (17%)
  waiting for transfers between devices  14.9 us (7%)
  blocking collectives  10.4 us (5%)
  loops' own time  4.54 us (2%)
    reduce_sum x64, other arithmetic, pull_toward(): radius_sq = jnp.sum(offset * offset, axis=0) + SOFTENING  37.7 us
    reduce_sum x64, other arithmetic, pull_toward(): return jnp.sum(offset * weight[None], axis=1)  36.7 us
    gather x32, local copies, waits for them, and re-layouts, near_block(): chosen = source_pool[:, block_list]  18.8 us
    all_to_all x2, waiting for transfers between devices, relocate(): lax.all_to_all(outgoing, 'member', split_axis=1, concat_axis=1, tiled=True)  14.9 us
    mul x64, other arithmetic, pull_toward(): weight = sources[3][:, None] * inverse * inverse * inverse  14.1 us
    all_to_all x2, starting transfers between devices, relocate(): lax.all_to_all(labels, 'member', split_axis=1, concat_axis=1, tiled=True)  12 us
    all_to_all x2, starting transfers between devices, relocate(): lax.all_to_all(outgoing, 'member', split_axis=1, concat_axis=1, tiled=True)  12 us
    all_to_all x2, starting transfers between devices, forces(): lax.all_to_all(outgoing, 'member', split_axis=1, concat_axis=1, tiled=True)  10.9 us
  transfers between devices with their start and end apart: 6, of which 2 were waited for; matrix products, arithmetic and copies ran while one was open for 63% of the time, Pallas kernels for 0%

commit v1 on v0

v1 whole, which is shorter than its diff:
```python
import functools

import jax
import jax.numpy as jnp
from jax import lax
from jax.experimental import pallas as pl
from jax.experimental.pallas import tpu as pltpu
from jax.sharding import PartitionSpec as P

BLOCK = 128
CELL = 16
SOFTENING = 0.01
TIMESTEP = 0.1
ROWS = 8
FEATS = 64
HALF = 0.5 * TIMESTEP


def parts_of(value):
    high = value.astype(jnp.bfloat16).astype(jnp.float32)
    rest = value - high
    middle = rest.astype(jnp.bfloat16).astype(jnp.float32)
    return high, middle, rest - middle


def rows_of(shape):
    return lax.broadcasted_iota(jnp.int32, shape, 0)


def source_features(block):
    row = rows_of(block.shape)
    mass = block[3:4]
    square = jnp.sum(jnp.where(row < 3, block * block, 0.0), axis=0, keepdims=True)
    tail = jnp.where(row == 3, square, jnp.where(row == 4, 1.0, 0.0))
    high, middle, low = parts_of(jnp.where(row < 3, block, tail))
    columns = jnp.concatenate([high, high, high, middle, middle, middle, low, low], axis=0)
    weighted = jnp.where(row < 3, block * mass, jnp.where(row == 3, mass, 0.0))
    moments = jnp.concatenate(parts_of(weighted) + (jnp.zeros_like(weighted),), axis=0)
    return jnp.transpose(columns).astype(jnp.bfloat16), moments.astype(jnp.bfloat16)


def target_features(block):
    row = rows_of(block.shape)
    square = jnp.sum(jnp.where(row < 3, block * block, 0.0), axis=0, keepdims=True)
    tail = jnp.where(row == 3, 1.0, jnp.where(row == 4, square + SOFTENING, 0.0))
    high, middle, low = parts_of(jnp.where(row < 3, -2.0 * block, tail))
    rows = jnp.concatenate([high, middle, low, high, middle, low, high, middle], axis=0)
    return rows.astype(jnp.bfloat16)


def moments_of(columns, moments, targets):
    radius_sq = jnp.dot(columns, targets, preferred_element_type=jnp.float32)
    inverse = lax.rsqrt(radius_sq)
    weight = (inverse * inverse * inverse).astype(jnp.bfloat16)
    return jnp.dot(moments, weight, preferred_element_type=jnp.float32)


def fold(sums):
    return sums[0:ROWS] + sums[ROWS : 2 * ROWS] + sums[2 * ROWS : 3 * ROWS]


def kernel(
    sizes,
    ints,
    position,
    velocity,
    mass,
    out_position,
    out_velocity,
    out_mass,
    half,
    speed,
    columns,
    moments,
    targets,
    far,
    far_columns,
    far_moments,
    let_out,
    let_in,
    cell_out,
    cell_in,
    move_out,
    move_in,
    let_send,
    let_recv,
    cell_send,
    cell_recv,
    move_send,
    move_recv,
):
    blocks, entries, members, groups, capacity, publish = sizes
    slots = members * capacity
    chunks = far_columns.shape[0]
    per_chunk = groups // chunks
    lengths_at = blocks * entries
    let_at = lengths_at + blocks
    cells_at = let_at + members
    order_at = cells_at + publish
    slot_at = order_at + 2 * slots
    group, member = lax.axis_index("group"), lax.axis_index("member")

    def peer(distance):
        return {"member": lax.rem(member + distance, members)}

    def group_peer(distance):
        return {"group": lax.rem(group + distance, groups)}

    mesh_id = pl.DeviceIdType.MESH
    barrier = pltpu.get_barrier_semaphore()
    for distance in range(1, members):
        pl.semaphore_signal(barrier, inc=1, device_id=peer(distance), device_id_type=mesh_id)
    for distance in range(1, groups):
        pl.semaphore_signal(barrier, inc=1, device_id=group_peer(distance), device_id_type=mesh_id)

    def let_copy(turn, distance):
        return pltpu.make_async_remote_copy(
            src_ref=let_out.at[turn, distance],
            dst_ref=let_in.at[turn, distance],
            send_sem=let_send.at[turn, distance],
            recv_sem=let_recv.at[turn, distance],
            device_id=peer(distance),
            device_id_type=mesh_id,
        )

    def cell_copy(turn, distance):
        return pltpu.make_async_remote_copy(
            src_ref=cell_out.at[turn],
            dst_ref=cell_in.at[turn, distance],
            send_sem=cell_send.at[turn, distance],
            recv_sem=cell_recv.at[turn, distance],
            device_id=group_peer(distance),
            device_id_type=mesh_id,
        )

    def move_copy(turn, distance):
        return pltpu.make_async_remote_copy(
            src_ref=move_out.at[turn, distance],
            dst_ref=move_in.at[turn, distance],
            send_sem=move_send.at[turn, distance],
            recv_sem=move_recv.at[turn, distance],
            device_id=peer(distance),
            device_id_type=mesh_id,
        )

    def arrived(turn, block):
        slot = ints[slot_at + turn * blocks + block]
        return move_in[turn, slot // capacity, slot % capacity]

    speed[...] = jnp.zeros_like(speed)
    half[...] = jnp.zeros_like(half)
    row = rows_of((ROWS, BLOCK))
    lane = lax.broadcasted_iota(jnp.int32, (ROWS, BLOCK), 1)

    for turn in range(2):

        def load_block(block, _):
            at = pl.ds(pl.multiple_of(block * BLOCK, BLOCK), BLOCK)
            if turn == 0:
                place, pace = position[:, at], velocity[:, at]
                heft = mass[pl.ds(block, 1), :]
            else:
                state = arrived(0, block)
                place, pace, heft = state[0:3], state[4:7], state[3:4]
            half[block, 0:3, :] = place + HALF * pace
            half[block, 3:4, :] = heft
            speed[block, 0:3, :] = pace
            return 0

        lax.fori_loop(0, blocks, load_block, 0, unroll=4)

        for distance in range(members):
            listed = ints[let_at + lax.rem(member + distance, members)]
            whole = half[listed]
            if distance == 0:
                let_in[turn, 0] = whole[0:4]
            else:
                let_out[turn, distance] = whole[0:4]
        if turn == 0:
            pl.semaphore_wait(barrier, members + groups - 2)
        for distance in range(1, members):
            let_copy(turn, distance).start()

        per_block = BLOCK // CELL
        offset = lax.rem(group, per_chunk) * publish
        found = jnp.zeros((ROWS, BLOCK), jnp.float32)
        for entry in range(publish):
            cell = ints[cells_at + entry]
            block = half[cell // per_block]
            heft = block[3:4]
            weighted = jnp.where(row < 3, block * heft, block)
            inside = lane // CELL == cell % per_block
            total = jnp.sum(jnp.where(inside, weighted, 0.0), axis=1, keepdims=True)
            found = jnp.where(lane == offset + entry, total, found)
        held = (lane >= offset) & (lane < offset + publish)
        heft = jnp.where(held, found[3:4], 1.0)
        found = jnp.where(row < 3, found / heft, found)
        if chunks > 1:
            cell_out[turn] = jnp.zeros_like(cell_out[turn])
        cell_out[turn, group // per_chunk] = found
        for distance in range(1, groups):
            cell_copy(turn, distance).start()

        def featurise(block, _):
            here = half[block]
            columns[block], moments[block] = source_features(here)
            targets[block] = target_features(here)
            return 0

        lax.fori_loop(0, blocks, featurise, 0, unroll=4)

        for distance in range(1, groups):
            cell_copy(turn, distance).wait_recv()
        for chunk in range(chunks):
            total = cell_in[turn, 1, chunk]
            for distance in range(2, groups):
                total = total + cell_in[turn, distance, chunk]
            far_columns[chunk], far_moments[chunk] = source_features(total)

        def far_pair(pair, _):
            two = jnp.concatenate([targets[2 * pair], targets[2 * pair + 1]], axis=1)
            total = moments_of(far_columns[0], far_moments[0], two)
            for chunk in range(1, chunks):
                total = total + moments_of(far_columns[chunk], far_moments[chunk], two)
            total = fold(total)
            far[2 * pair], far[2 * pair + 1] = total[:, :BLOCK], total[:, BLOCK:]
            return 0

        lax.fori_loop(0, blocks // 2, far_pair, 0, unroll=2)

        for distance in range(1, members):
            let_copy(turn, distance).wait_recv()

        def featurise_listed(distance, _):
            spread = jnp.concatenate(
                [let_in[turn, distance], jnp.zeros((4, BLOCK), jnp.float32)], axis=0
            )
            columns[blocks + distance], moments[blocks + distance] = source_features(spread)
            return 0

        lax.fori_loop(0, members, featurise_listed, 0, unroll=2)

        width = 4 if capacity % 4 == 0 else capacity

        def near(distance, into):
            def some(step, _):
                results = []
                for inner in range(width):
                    rank = step * width + inner
                    block = ints[order_at + turn * slots + distance * capacity + rank]
                    goal = targets[block]
                    length = ints[lengths_at + block]
                    total = None
                    for entry in range(entries):
                        source = ints[block * entries + entry]
                        live = (entry < length).astype(jnp.float32).astype(jnp.bfloat16)
                        term = moments_of(columns[source], moments[source] * live, goal)
                        total = term if total is None else total + term
                    sums = fold(total) + far[block]
                    here = half[block]
                    pull = jnp.where(row < 3, sums - here * sums[3:4], 0.0)
                    pace = speed[block] + TIMESTEP * pull
                    results.append((rank, here + HALF * pace, pace))
                for rank, place, pace in results:
                    into[turn, distance, rank, 0:4, :] = place[0:4]
                    into[turn, distance, rank, 4:7, :] = pace[0:3]
                return 0

            lax.fori_loop(0, capacity // width, some, 0)

        def send_away(index, _):
            swing = (index + 1) // 2
            distance = members // 2 + jnp.where(index % 2 == 1, -swing, swing)
            near(distance, move_out)
            move_copy(turn, distance).start()
            return 0

        lax.fori_loop(0, members - 1, send_away, 0)
        near(0, move_in)
        for distance in range(1, members):
            move_copy(turn, distance).wait_recv()

    def unload(block, _):
        at = pl.ds(pl.multiple_of(block * BLOCK, BLOCK), BLOCK)
        state = arrived(1, block)
        out_position[:, at] = state[0:3]
        out_velocity[:, at] = state[4:7]
        out_mass[pl.ds(block, 1), :] = state[3:4]
        return 0

    lax.fori_loop(0, blocks, unload, 0, unroll=4)
    for turn in range(2):
        for distance in range(1, members):
            let_copy(turn, distance).wait_send()
            move_copy(turn, distance).wait_send()
        for distance in range(1, groups):
            cell_copy(turn, distance).wait_send()


def shards(position, velocity, mass, neighbours, list_length, let_list, cell_list, destination):
    members, groups = lax.axis_size("member"), lax.axis_size("group")
    member = lax.axis_index("member")
    blocks, entries = neighbours.shape
    publish = cell_list.shape[1]
    capacity = (blocks + members - 1) // members
    slots = members * capacity
    chunks = max(1, groups * publish // BLOCK)

    shift = (destination - member) % members
    number = jnp.arange(blocks, dtype=jnp.int32)
    same = (shift[:, :, None] == shift[:, None, :]) & (number[None, :] < number[:, None])
    slot = shift * capacity + jnp.sum(same, axis=2, dtype=jnp.int32)
    hit = slot[:, None, :] == jnp.arange(slots, dtype=jnp.int32)[None, :, None]
    order = jnp.sum(jnp.where(hit, number[None, None, :], 0), axis=2, dtype=jnp.int32)
    pool = jnp.where(
        neighbours < blocks, neighbours, blocks + (member - (neighbours - blocks)) % members
    )
    ints = jnp.concatenate(
        [
            pool.reshape(-1),
            list_length,
            let_list.reshape(-1),
            cell_list.reshape(-1),
            order.reshape(-1),
            slot.reshape(-1),
        ]
    )
    vmem = pl.BlockSpec(memory_space=pltpu.VMEM)
    f32, bf16 = jnp.float32, jnp.bfloat16
    pool_size = blocks + members
    dma = pltpu.SemaphoreType.DMA
    results = pl.pallas_call(
        functools.partial(kernel, (blocks, entries, members, groups, capacity, publish)),
        out_shape=(
            jax.ShapeDtypeStruct(position.shape, f32),
            jax.ShapeDtypeStruct(velocity.shape, f32),
            jax.ShapeDtypeStruct((blocks, BLOCK), f32),
        ),
        in_specs=[pl.BlockSpec(memory_space=pltpu.SMEM), vmem, vmem, vmem],
        out_specs=(vmem, vmem, vmem),
        scratch_shapes=[
            pltpu.VMEM((blocks, ROWS, BLOCK), f32),
            pltpu.VMEM((blocks, ROWS, BLOCK), f32),
            pltpu.VMEM((pool_size, BLOCK, FEATS), bf16),
            pltpu.VMEM((pool_size, 4 * ROWS, BLOCK), bf16),
            pltpu.VMEM((blocks, FEATS, BLOCK), bf16),
            pltpu.VMEM((blocks, ROWS, BLOCK), f32),
            pltpu.VMEM((chunks, BLOCK, FEATS), bf16),
            pltpu.VMEM((chunks, 4 * ROWS, BLOCK), bf16),
            pltpu.VMEM((2, members, 4, BLOCK), f32),
            pltpu.VMEM((2, members, 4, BLOCK), f32),
            pltpu.VMEM((2, chunks, ROWS, BLOCK), f32),
            pltpu.VMEM((2, groups, chunks, ROWS, BLOCK), f32),
            pltpu.VMEM((2, members, capacity, 7, BLOCK), f32),
            pltpu.VMEM((2, members, capacity, 7, BLOCK), f32),
            dma((2, members)),
            dma((2, members)),
            dma((2, groups)),
            dma((2, groups)),
            dma((2, members)),
            dma((2, members)),
        ],
        compiler_params=pltpu.CompilerParams(
            collective_id=0, has_side_effects=True, vmem_limit_bytes=48 * 1024 * 1024
        ),
        name="two_steps",
    )(ints, position, velocity, mass.reshape(blocks, BLOCK))
    return results[0], results[1], results[2].reshape(-1)


def solution(mesh):
    shared = ("group", "member")
    return jax.shard_map(
        shards,
        mesh=mesh,
        in_specs=(
            P(None, shared),
            P(None, shared),
            P(shared),
            P(shared, None),
            P(shared),
            P(shared, None),
            P(shared, None),
            P(None, shared),
        ),
        out_specs=(P(None, shared), P(None, shared), P(shared)),
        check_vma=False,
    )
```

time: 204 us -> 81.8 us (0.40)
  other arithmetic: 99.9 us -> 0.34 us
  Pallas kernels: 0 us -> 75.1 us
  starting transfers between devices: 34.8 us -> 0 us
  local copies, waits for them, and re-layouts: 36.1 us -> 5.43 us
  waiting for transfers between devices: 14.9 us -> 0 us
  blocking collectives: 10.4 us -> 0 us
  loops' own time: 4.54 us -> 0 us
    reduce_sum x134 -> x2, other arithmetic: 75.6 us -> 0.29 us  [the longest x1 0.18 us: shards(): slot = shift * capacity + jnp.sum(same, axis=2, dtype=jnp.int32)]
    pallas_call x0 -> x1, Pallas kernels: none -> 75.1 us  [shards(): pl.pallas_call(functools.partial(kernel, (blocks, entries, members, group...]
    all_to_all x6 -> x0, starting transfers between devices: 34.8 us -> none  [the longest x2 12 us: relocate(): lax.all_to_all(labels, 'member', split_axis=1, concat_axis=1, tiled=True)]
    gather x40 -> x0, local copies, waits for them, and re-layouts: 23.9 us -> none  [the longest x32 18.8 us: near_block(): chosen = source_pool[:, block_list]]
    mul x101 -> x0, other arithmetic: 17.4 us -> none  [the longest x64 14.1 us: pull_toward(): weight = sources[3][:, None] * inverse * inverse * inverse]
    all_to_all x6 -> x0, waiting for transfers between devices: 14.9 us -> none  [the longest x2 14.9 us: relocate(): lax.all_to_all(outgoing, 'member', split_axis=1, concat_axis=1, tiled=True)]
    all_gather x2 -> x0, blocking collectives: 10.4 us -> none  [forces(): piece = lax.all_gather(published, 'group', axis=1, tiled=True)]
    unnamed x18 -> x19, local copies, waits for them, and re-layouts: 0.36 us -> 4.98 us
  transfers between devices with their start and end apart: 6 -> 0, of which waited for: 2 -> 0; matrix products, arithmetic and copies ran while one was open for 63% -> 0% of each run, Pallas kernels for 0% -> 0%
where the time goes in v1:
time: 81.8 us; the launch traced here: 81.5 us
  Pallas kernels  75.1 us (92%)
  local copies, waits for them, and re-layouts  5.43 us (7%)
    pallas_call x1, Pallas kernels, shards(): pl.pallas_call(functools.partial(kernel, (blocks, entries, members, group...  75.1 us
    unnamed x19, local copies, waits for them, and re-layouts  4.98 us

profile of v1, /device:TPU:0, one launch (start us, length us, event | category | flops | bytes accessed | tf_op | source)
XLA Modules:
  0.0 81.5 jit_solution(11425493381625055352)
XLA Ops:
  0.6 0.0 copy-start.3
  0.6 0.0 copy-start.4
  0.7 0.7 copy-done.3
  1.3 0.0 copy-done.4
  1.4 0.2 convert_reduce_fusion
  1.6 0.1 reshape.46
  1.6 0.1 select_reduce_fusion
  1.8 0.1 reshape.45
  1.8 0.1 copy.12
  1.9 0.0 copy-start.5
  1.9 0.0 copy-start.6
  2.0 0.0 copy-start.7
  2.0 0.1 reshape.42
  2.1 0.5 copy-done.5
  2.6 0.0 copy-done.6
  2.6 0.0 copy-done.7
  2.6 0.1 concatenate.3.ints
  2.7 0.0 copy-done.2
  2.7 0.9 %copy-done = f32[3,8192]{1,0:T(4,128)S(1)} copy-done((f32[3,8192]{1,0:T(4,128)S(1)}, f32[3,8192]{1,0:T(4,128)}, u32[]{:S(2)}) %copy-start) | copy-done | bytes 98328
  3.6 0.9 %copy-done.1 = f32[3,8192]{1,0:T(4,128)S(1)} copy-done((f32[3,8192]{1,0:T(4,128)S(1)}, f32[3,8192]{1,0:T(4,128)}, u32[]{:S(2)}) %copy-start.1) | copy-done | bytes 98328
  4.5 75.1 %two_steps.1 = (f32[3,8192]{1,0:T(4,128)S(1)}, f32[3,8192]{1,0:T(4,128)S(1)}, f32[64,128]{1,0:T(8,128)S(1)}) custom-call(s32[616]{0:T(1024)S(1)} %concatenate.3.ints, f32[3,8192]{1,0:T(4,128)S(1)} %copy-done, f32[3,8192]{1,0:T(4,128)S(1)} %copy-done.1, f32[64,128]{1,0:T(8,128)S(1)} %bitcast.4), custom_call_target="tpu_custom_call" | custom-call | tf_op jit(solution)/shard_map/two_steps/pallas_call | solution.py:332
  79.6 0.7 copy.16
  80.3 0.7 copy.17
  80.9 0.6 copy.18
  (7 shorter events, 0.1 us)
Async XLA Ops:
  0.6 0.7 copy-start.3
  0.6 0.7 copy-start.4
  1.8 0.9 %copy-start.2 = (f32[8192]{0:T(1024)S(1)}, f32[8192]{0:T(1024)}, u32[]{:S(2)}) copy-start(f32[8192]{0:T(1024)} %param.10) | copy-start | bytes 98308
  1.9 0.7 copy-start.5
  1.9 0.7 copy-start.6
  2.0 0.7 copy-start.7
  2.7 0.9 %copy-start = (f32[3,8192]{1,0:T(4,128)S(1)}, f32[3,8192]{1,0:T(4,128)}, u32[]{:S(2)}) copy-start(f32[3,8192]{1,0:T(4,128)} %position.1) | copy-start | bytes 294916
  3.6 0.9 %copy-start.1 = (f32[3,8192]{1,0:T(4,128)S(1)}, f32[3,8192]{1,0:T(4,128)}, u32[]{:S(2)}) copy-start(f32[3,8192]{1,0:T(4,128)} %velocity.1) | copy-start | bytes 294916
